TPU v7x, 32 devices: a whole 2x2x4 slice. The times are simulated.
32 devices in a mesh: groups: 2 (over x), ep: 16 (over z, y, core).
Axes of the slice: x: 2, y: 2, z: 4, core: 2. Of those that a mesh axis runs over, the one named last changes fastest.
Arguments:
- tokens: bfloat16 [512, 3072], P(('groups', 'ep')), parts along dimension 0, may hold values from -6 to 6
- routes: int32 [512, 2], P(('groups', 'ep')), parts along dimension 0, may hold values from 0 to 3, all different within a row
- route_weights: float32 [512, 2], P(('groups', 'ep')), parts along dimension 0, may hold values from 0.1 to 1
- live_counts: int32 [32], P(('groups', 'ep')), parts along dimension 0, may hold values from 8 to 16, as said below
- w_gate: bfloat16 [3072, 32768], P(None, 'ep'), may hold values from -0.109375 to 0.109375
- w_up: bfloat16 [3072, 32768], P(None, 'ep'), may hold values from -0.109375 to 0.109375
- w_down: bfloat16 [32768, 3072], P('ep'), may hold values from -0.0625 to 0.0625
Outputs:
- mixed: bfloat16 [512, 3072], P(('groups', 'ep')), parts along dimension 0
There are 2 independent parts, one for each index of `groups`. A program takes and returns all parts, laid end to end along the dimension named above; an argument that names none is the same for every part. Nothing has to cross between parts.
Inputs may be any that keep to these rules, and one draw needn't show every extreme that they name: `routes`: each token names two different experts. The live tokens of a device are its first live_counts rows; some device has all 16 live and some has 8.
All inputs are finite; a program needn't handle non-finite values.
Results may differ from a plain program's by a relative error of at most 0.0057.
Values may be sent and summed in bfloat16 or wider, within the bound.
A program may use at most 128 MiB of HBM per device.

v0:
```python
import jax
import jax.numpy as jnp
from jax import lax
from jax.sharding import PartitionSpec as P

EXPERTS = 4


def expert_rows(row_block, w_gate, w_up, w_down):
    gate = jnp.dot(row_block, w_gate, preferred_element_type=jnp.float32)
    upward = jnp.dot(row_block, w_up, preferred_element_type=jnp.float32)
    hidden = (jax.nn.silu(gate) * upward).astype(jnp.bfloat16)
    return jnp.dot(hidden, w_down, preferred_element_type=jnp.float32).astype(jnp.bfloat16)


def local(tokens, routes, route_weights, live_counts, w_gate, w_up, w_down):
    devices = lax.axis_size("ep")
    partners = devices // EXPERTS
    tok_rows, features = tokens.shape
    all_rows = devices * tok_rows
    is_live = jnp.arange(tok_rows, dtype=jnp.int32) < live_counts[0]
    chosen = (routes[:, :, None] == jnp.arange(EXPERTS, dtype=jnp.int32)[None, None, :]) & is_live[
        :, None, None
    ]
    assigned = chosen.reshape(tok_rows * 2, EXPERTS).astype(jnp.int32)
    earlier = jnp.cumsum(assigned, axis=0) - assigned
    slot_index = jnp.sum(earlier * assigned, axis=1).reshape(tok_rows, 2)
    target = jnp.where(is_live[:, None], routes * tok_rows + slot_index, -1)
    select = jnp.any(
        jnp.arange(EXPERTS * tok_rows, dtype=jnp.int32)[:, None, None] == target[None, :, :], axis=2
    )
    outbox = jnp.dot(
        select.astype(jnp.bfloat16), tokens, preferred_element_type=jnp.float32
    ).astype(jnp.bfloat16)
    outbox = outbox.reshape(EXPERTS, tok_rows, features)
    outgoing = jnp.broadcast_to(outbox[:, None], (EXPERTS, partners, tok_rows, features)).reshape(
        devices, tok_rows, features
    )
    received = lax.all_to_all(outgoing, "ep", split_axis=0, concat_axis=0, tiled=True)
    flat_rows = received.reshape(all_rows, features)
    partial_value = expert_rows(flat_rows, w_gate, w_up, w_down)
    returned = lax.all_to_all(
        partial_value.reshape(devices, tok_rows, features),
        "ep",
        split_axis=0,
        concat_axis=0,
        tiled=True,
    )
    summed = jnp.sum(
        returned.reshape(EXPERTS, partners, tok_rows, features).astype(jnp.float32), axis=1
    )
    gathered = summed.reshape(EXPERTS * tok_rows, features)
    picked = gathered[jnp.maximum(target, 0)]
    mixed = (
        route_weights[:, 0][:, None] * picked[:, 0] + route_weights[:, 1][:, None] * picked[:, 1]
    )
    mixed = jnp.where(is_live[:, None], mixed, jnp.float32(0.0))
    return mixed.astype(jnp.bfloat16)


def solution(mesh):
    in_specs = (
        P(("groups", "ep"), None),
        P(("groups", "ep"), None),
        P(("groups", "ep"), None),
        P(("groups", "ep")),
        P(None, "ep"),
        P(None, "ep"),
        P("ep", None),
    )
    out_specs = P(("groups", "ep"), None)
    return jax.shard_map(local, mesh=mesh, in_specs=in_specs, out_specs=out_specs, check_vma=False)
```

profile of v0, /device:TPU:15, one launch (start us, length us, event | category | flops | bytes accessed | tf_op | source)
XLA Modules:
  0.0 114.2 jit_solution(10619593889007973785)
XLA Ops:
  0.0 0.0 copy-start
  0.7 0.1 broadcast_in_dim.42.clone
  0.8 0.1 and.11
  0.9 0.8 copy.24
  1.6 0.1 eq.30
  1.7 0.1 fusion.8
  1.8 0.1 reduce_window_sum.11
  1.9 0.2 select_reduce_fusion
  2.0 0.1 reshape.33
  2.1 0.1 copy.26
  2.2 0.7 broadcast_maximum_fusion
  2.9 0.1 fusion.6
  3.0 0.0 copy-done
  3.0 0.3 convolution_convert_fusion.1
  3.3 0.2 broadcast_in_dim.45
  3.5 42.4 %all_to_all.10 = bf16[16,16,3072]{2,1,0:T(8,128)(2,1)S(1)} all-to-all(bf16[16,16,3072]{2,1,0:T(8,128)(2,1)S(1)} %bitcast.38), channel_id=1, replica_groups=mesh['groups'=2,'ep'=16] {'ep'}, dimensions={0} | all-to-all | bytes 3145728 | tf_op jit(solution)/shard_map/all_to_all | solution.py:39
  45.9 7.8 %fusion.11 = f32[256,2048]{1,0:T(8,128)} fusion(bf16[256,3072]{1,0:T(8,128)(2,1)S(1)} %bitcast.39, bf16[3072,2048]{1,0:T(8,128)(2,1)} %param.11), kind=kOutput, calls=%fused_computation.27 | convolution fusion | flops 3221225472 | bytes 16252928 | tf_op jit(solution)/shard_map/dot_general | solution.py:10
  53.7 16.9 %convolution_convert_fusion = bf16[256,3072]{1,0:T(8,128)(2,1)} fusion(bf16[2048,3072]{1,0:T(8,128)(2,1)} %param.13, bf16[256,3072]{1,0:T(8,128)(2,1)S(1)} %bitcast.40, bf16[3072,2048]{1,0:T(8,128)(2,1)} %param.12, f32[256,2048]{1,0:T(8,128)} %fusion.11), kind=kOutput, calls=%fused_computation.1 | convolution fusion | flops 6446383104 | bytes 30408704 | tf_op jit(solution)/shard_map/dot_general | solution.py:13
  70.6 0.0 copy-start.1
  70.6 5.2 %all-to-all-start.1 = ((bf16[16,16,3072]{2,1,0:T(8,128)(2,1)}), bf16[16,16,3072]{2,1,0:T(8,128)(2,1)S(1)}, u32[]{:S(2)}, u32[]{:S(2)}) async-start(bf16[16,16,3072]{2,1,0:T(8,128)(2,1)} %bitcast.5), calls=%async_computation.1 | async-start | bytes 3145728 | tf_op jit(solution)/shard_map/all_to_all | solution.py:42
  75.7 0.1 copy.27
  75.8 0.1 reshape.41
  75.9 0.0 copy-done.1
  76.0 36.0 %all-to-all-done.1 = bf16[16,16,3072]{2,1,0:T(8,128)(2,1)S(1)} async-done(((bf16[16,16,3072]{2,1,0:T(8,128)(2,1)}), bf16[16,16,3072]{2,1,0:T(8,128)(2,1)S(1)}, u32[]{:S(2)}, u32[]{:S(2)}) %all-to-all-start.1) | async-done | bytes 1572896 | tf_op jit(solution)/shard_map/all_to_all | solution.py:42
  111.9 0.2 convert_reduce_fusion
  112.2 0.7 gather_fusion
  112.9 0.2 reshape.40
  113.1 0.3 fusion.10
  113.4 0.8 fusion.4
  (3 shorter events, 0.0 us)
Async XLA Ops:
  0.0 3.0 %copy-start = (bf16[16,3072]{1,0:T(8,128)(2,1)S(1)}, bf16[16,3072]{1,0:T(8,128)(2,1)}, u32[]{:S(2)}) copy-start(bf16[16,3072]{1,0:T(8,128)(2,1)} %param.7) | copy-start | bytes 294916
  70.6 5.4 %copy-start.1 = (f32[16,2]{0,1:T(2,128)S(1)}, f32[16,2]{0,1:T(2,128)}, u32[]{:S(2)}) copy-start(f32[16,2]{0,1:T(2,128)} %param.9) | copy-start | bytes 388
  70.6 41.4 %all-to-all-start.1 = ((bf16[16,16,3072]{2,1,0:T(8,128)(2,1)}), bf16[16,16,3072]{2,1,0:T(8,128)(2,1)S(1)}, u32[]{:S(2)}, u32[]{:S(2)}) async-start(bf16[16,16,3072]{2,1,0:T(8,128)(2,1)} %bitcast.5), calls=%async_computation.1 | async-start | bytes 3145728 | tf_op jit(solution)/shard_map/all_to_all | solution.py:42
where the time goes:
time: 114 us
  blocking collectives  42.4 us (37%)
  waiting for transfers between devices  36 us (32%)
  matrix products  25 us (22%)
  starting transfers between devices  5.18 us (5%)
  local copies, waits for them, and re-layouts  2.77 us (2%)
  other arithmetic  2.13 us (2%)
    all_to_all x1, blocking collectives, local(): lax.all_to_all(outgoing, 'ep', split_axis=0, concat_axis=0, tiled=True)  42.4 us
    all_to_all x1, waiting for transfers between devices, local(): lax.all_to_all(partial_value.reshape(devices, tok_rows, features), 'ep',...  36 us
    dot_general x1, matrix products, expert_rows(): jnp.dot(hidden, w_down, preferred_element_type=jnp.float32)  16.9 us
    dot_general x1, matrix products, expert_rows(): gate = jnp.dot(row_block, w_gate, preferred_element_type=jnp.float32)  7.78 us
    all_to_all x1, starting transfers between devices, local(): lax.all_to_all(partial_value.reshape(devices, tok_rows, features), 'ep',...  5.18 us
  transfers between devices with their start and end apart: 1, of which 1 were waited for; matrix products, arithmetic and copies ran while one was open for 0% of the time, Pallas kernels for 0%

commit v1 on v0

--- a/solution.py
+++ b/solution.py
@@ -36,7 +36,19 @@
     outgoing = jnp.broadcast_to(outbox[:, None], (EXPERTS, partners, tok_rows, features)).reshape(
         devices, tok_rows, features
     )
-    received = lax.all_to_all(outgoing, "ep", split_axis=0, concat_axis=0, tiled=True)
+    ways, here = (lax.axis_size("ep"), lax.axis_index("ep"))
+    width = outgoing.shape[0] // ways
+    shape = list(outgoing.shape)
+    shape[0] = width
+    height = shape[0]
+    shape[0] = height * ways
+    full = jnp.zeros(shape, outgoing.dtype)
+    for mask in range(ways):
+        part = lax.dynamic_slice_in_dim(outgoing, (here ^ mask) * width, width, axis=0)
+        if mask:
+            part = lax.ppermute(part, "ep", [(d, d ^ mask) for d in range(ways)])
+        full = lax.dynamic_update_slice_in_dim(full, part, (here ^ mask) * height, axis=0)
+    received = full
     flat_rows = received.reshape(all_rows, features)
     partial_value = expert_rows(flat_rows, w_gate, w_up, w_down)
     returned = lax.all_to_all(

time: 114 us -> 118 us (1.035)
  blocking collectives: 42.4 us -> 0 us
  waiting for transfers between devices: 36 us -> 61 us
  starting transfers between devices: 5.18 us -> 25 us
    all_to_all x1 -> x0, blocking collectives: 42.4 us -> none  [local(): lax.all_to_all(outgoing, 'ep', split_axis=0, concat_axis=0, tiled=True)]
    ppermute x0 -> x15, waiting for transfers between devices: none -> 25 us  [local(): part = lax.ppermute(part, 'ep', [(d, d ^ mask) for d in range(ways)])]
    ppermute x0 -> x15, starting transfers between devices: none -> 19.1 us  [local(): part = lax.ppermute(part, 'ep', [(d, d ^ mask) for d in range(ways)])]
  transfers between devices with their start and end apart: 1 -> 16, of which waited for: 1 -> 10; matrix products, arithmetic and copies ran while one was open for 0% -> 0% of each run, Pallas kernels for 0% -> 0%
where the time goes in v1:
time: 118 us; the launch traced here: 117 us
  waiting for transfers between devices  61 us (52%)
  matrix products  25 us (21%)
  starting transfers between devices  25 us (21%)
  local copies, waits for them, and re-layouts  3.32 us (3%)
  other arithmetic  2.14 us (2%)
    all_to_all x1, waiting for transfers between devices, local(): lax.all_to_all(partial_value.reshape(devices, tok_rows, features), 'ep',...  36 us
    ppermute x15, waiting for transfers between devices, local(): part = lax.ppermute(part, 'ep', [(d, d ^ mask) for d in range(ways)])  25 us
    ppermute x15, starting transfers between devices, local(): part = lax.ppermute(part, 'ep', [(d, d ^ mask) for d in range(ways)])  19.1 us
    dot_general x1, matrix products, expert_rows(): jnp.dot(hidden, w_down, preferred_element_type=jnp.float32)  16.9 us
    dot_general x1, matrix products, expert_rows(): gate = jnp.dot(row_block, w_gate, preferred_element_type=jnp.float32)  7.77 us
    all_to_all x1, starting transfers between devices, local(): lax.all_to_all(partial_value.reshape(devices, tok_rows, features), 'ep',...  5.93 us
  transfers between devices with their start and end apart: 16, of which 10 were waited for; matrix products, arithmetic and copies ran while one was open for 0% of the time, Pallas kernels for 0%

profile of v1, /device:TPU:15, one launch (start us, length us, event | category | flops | bytes accessed | tf_op | source)
XLA Modules:
  0.0 117.3 jit_solution(16067100868138944885)
XLA Ops:
  0.7 0.1 broadcast_in_dim.46.clone
  0.8 0.1 and.12
  0.9 0.8 copy.24
  1.6 0.1 eq.30
  1.7 0.1 fusion.8
  1.9 0.2 select_reduce_fusion
  2.0 0.1 reshape.33
  2.1 0.1 copy.26
  2.2 0.7 broadcast_maximum_fusion
  2.9 0.1 fusion.6
  3.0 0.3 convolution_convert_fusion.1
  3.3 0.2 broadcast_in_dim.49
  3.5 0.2 broadcast_in_dim.45
  3.7 0.2 constant_dynamic-slice_fusion
  3.9 0.7 collective-permute-start
  4.7 0.3 collective-permute-start.1
  4.9 1.5 %collective-permute-start.2 = (bf16[1,16,3072]{2,1,0:T(8,128)(2,1)S(1)}, bf16[1,16,3072]{2,1,0:T(8,128)(2,1)S(1)}, u32[]{:S(2)}, u32[]{:S(2)}) collective-permute-start(bf16[1,16,3072]{2,1,0:T(8,128)(2,1)S(1)} %get-tuple-element.19), channel_id=1, source_target_pairs={{0,3},{1,2},{2,1},{3,0},{4,7},{5,6},{6,5},{7,4},{8,11},{9,10},{10,... | collective-permute-start | bytes 294920 | tf_op jit(solution)/shard_map/ppermute | solution.py:49
  6.4 0.2 collective-permute-start.3
  6.5 1.6 %collective-permute-start.4 = (bf16[1,16,3072]{2,1,0:T(8,128)(2,1)S(1)}, bf16[1,16,3072]{2,1,0:T(8,128)(2,1)S(1)}, u32[]{:S(2)}, u32[]{:S(2)}) collective-permute-start(bf16[1,16,3072]{2,1,0:T(8,128)(2,1)S(1)} %get-tuple-element.17), channel_id=1, source_target_pairs={{0,5},{1,4},{2,7},{3,6},{4,1},{5,0},{6,3},{7,2},{8,13},{9,12},{10,... | collective-permute-start | bytes 294920 | tf_op jit(solution)/shard_map/ppermute | solution.py:49
  8.2 0.1 collective-permute-start.5
  8.3 0.7 collective-permute-done.1
  9.0 1.8 %collective-permute-start.6 = (bf16[1,16,3072]{2,1,0:T(8,128)(2,1)S(1)}, bf16[1,16,3072]{2,1,0:T(8,128)(2,1)S(1)}, u32[]{:S(2)}, u32[]{:S(2)}) collective-permute-start(bf16[1,16,3072]{2,1,0:T(8,128)(2,1)S(1)} %get-tuple-element.15), channel_id=1, source_target_pairs={{0,7},{1,6},{2,5},{3,4},{4,3},{5,2},{6,1},{7,0},{8,15},{9,14},{10,... | collective-permute-start | bytes 294920 | tf_op jit(solution)/shard_map/ppermute | solution.py:49
  10.9 0.7 collective-permute-done.2
  11.6 2.3 %collective-permute-start.7 = (bf16[1,16,3072]{2,1,0:T(8,128)(2,1)S(1)}, bf16[1,16,3072]{2,1,0:T(8,128)(2,1)S(1)}, u32[]{:S(2)}, u32[]{:S(2)}) collective-permute-start(bf16[1,16,3072]{2,1,0:T(8,128)(2,1)S(1)} %get-tuple-element.14), channel_id=1, source_target_pairs={{0,8},{1,9},{2,10},{3,11},{4,12},{5,13},{6,14},{7,15},{8,0},{9,1},... | collective-permute-start | bytes 294920 | tf_op jit(solution)/shard_map/ppermute | solution.py:49
  13.9 0.4 collective-permute-start.8
  14.4 2.1 %collective-permute-start.9 = (bf16[1,16,3072]{2,1,0:T(8,128)(2,1)S(1)}, bf16[1,16,3072]{2,1,0:T(8,128)(2,1)S(1)}, u32[]{:S(2)}, u32[]{:S(2)}) collective-permute-start(bf16[1,16,3072]{2,1,0:T(8,128)(2,1)S(1)} %get-tuple-element.12), channel_id=1, source_target_pairs={{0,10},{1,11},{2,8},{3,9},{4,14},{5,15},{6,12},{7,13},{8,2},{9,3},... | collective-permute-start | bytes 294920 | tf_op jit(solution)/shard_map/ppermute | solution.py:49
  16.5 5.0 %collective-permute-start.10 = (bf16[1,16,3072]{2,1,0:T(8,128)(2,1)S(1)}, bf16[1,16,3072]{2,1,0:T(8,128)(2,1)S(1)}, u32[]{:S(2)}, u32[]{:S(2)}) collective-permute-start(bf16[1,16,3072]{2,1,0:T(8,128)(2,1)S(1)} %get-tuple-element.11), channel_id=1, source_target_pairs={{0,11},{1,10},{2,9},{3,8},{4,15},{5,14},{6,13},{7,12},{8,3},{9,2},... | collective-permute-start | bytes 294920 | tf_op jit(solution)/shard_map/ppermute | solution.py:49
  21.6 0.6 collective-permute-start.11
  22.2 0.1 collective-permute-start.12
  22.3 7.6 %collective-permute-done.8 = bf16[1,16,3072]{2,1,0:T(8,128)(2,1)S(1)} collective-permute-done((bf16[1,16,3072]{2,1,0:T(8,128)(2,1)S(1)}, bf16[1,16,3072]{2,1,0:T(8,128)(2,1)S(1)}, u32[]{:S(2)}, u32[]{:S(2)}) %collective-permute-start.8) | collective-permute-done | bytes 98336 | tf_op jit(solution)/shard_map/ppermute | solution.py:49
  30.0 2.1 %collective-permute-done.9 = bf16[1,16,3072]{2,1,0:T(8,128)(2,1)S(1)} collective-permute-done((bf16[1,16,3072]{2,1,0:T(8,128)(2,1)S(1)}, bf16[1,16,3072]{2,1,0:T(8,128)(2,1)S(1)}, u32[]{:S(2)}, u32[]{:S(2)}) %collective-permute-start.9) | collective-permute-done | bytes 98336 | tf_op jit(solution)/shard_map/ppermute | solution.py:49
  32.1 2.3 %collective-permute-start.14 = (bf16[1,16,3072]{2,1,0:T(8,128)(2,1)S(1)}, bf16[1,16,3072]{2,1,0:T(8,128)(2,1)S(1)}, u32[]{:S(2)}, u32[]{:S(2)}) collective-permute-start(bf16[1,16,3072]{2,1,0:T(8,128)(2,1)S(1)} %get-tuple-element.7), channel_id=1, source_target_pairs={{0,15},{1,14},{2,13},{3,12},{4,11},{5,10},{6,9},{7,8},{8,7},{9,6},... | collective-permute-start | bytes 294920 | tf_op jit(solution)/shard_map/ppermute | solution.py:49
  34.4 2.8 %collective-permute-done.10 = bf16[1,16,3072]{2,1,0:T(8,128)(2,1)S(1)} collective-permute-done((bf16[1,16,3072]{2,1,0:T(8,128)(2,1)S(1)}, bf16[1,16,3072]{2,1,0:T(8,128)(2,1)S(1)}, u32[]{:S(2)}, u32[]{:S(2)}) %collective-permute-start.10) | collective-permute-done | bytes 98336 | tf_op jit(solution)/shard_map/ppermute | solution.py:49
  37.2 4.4 %collective-permute-done.11 = bf16[1,16,3072]{2,1,0:T(8,128)(2,1)S(1)} collective-permute-done((bf16[1,16,3072]{2,1,0:T(8,128)(2,1)S(1)}, bf16[1,16,3072]{2,1,0:T(8,128)(2,1)S(1)}, u32[]{:S(2)}, u32[]{:S(2)}) %collective-permute-start.11) | collective-permute-done | bytes 98336 | tf_op jit(solution)/shard_map/ppermute | solution.py:49
  41.6 2.6 %collective-permute-done.12 = bf16[1,16,3072]{2,1,0:T(8,128)(2,1)S(1)} collective-permute-done((bf16[1,16,3072]{2,1,0:T(8,128)(2,1)S(1)}, bf16[1,16,3072]{2,1,0:T(8,128)(2,1)S(1)}, u32[]{:S(2)}, u32[]{:S(2)}) %collective-permute-start.12) | collective-permute-done | bytes 98336 | tf_op jit(solution)/shard_map/ppermute | solution.py:49
  44.2 1.6 %collective-permute-done.13 = bf16[1,16,3072]{2,1,0:T(8,128)(2,1)S(1)} collective-permute-done((bf16[1,16,3072]{2,1,0:T(8,128)(2,1)S(1)}, bf16[1,16,3072]{2,1,0:T(8,128)(2,1)S(1)}, u32[]{:S(2)}, u32[]{:S(2)}) %collective-permute-start.13) | collective-permute-done | bytes 98336 | tf_op jit(solution)/shard_map/ppermute | solution.py:49
  45.8 2.5 %collective-permute-done.14 = bf16[1,16,3072]{2,1,0:T(8,128)(2,1)S(1)} collective-permute-done((bf16[1,16,3072]{2,1,0:T(8,128)(2,1)S(1)}, bf16[1,16,3072]{2,1,0:T(8,128)(2,1)S(1)}, u32[]{:S(2)}, u32[]{:S(2)}) %collective-permute-start.14) | collective-permute-done | bytes 98336 | tf_op jit(solution)/shard_map/ppermute | solution.py:49
  48.2 7.8 %fusion.13 = f32[256,2048]{1,0:T(8,128)} fusion(bf16[256,3072]{1,0:T(8,128)(2,1)S(1)} %bitcast.39, bf16[3072,2048]{1,0:T(8,128)(2,1)} %param.11), kind=kOutput, calls=%fused_computation.59 | convolution fusion | flops 3221225472 | bytes 16252928 | tf_op jit(solution)/shard_map/dot_general | solution.py:10
  56.0 16.9 %convolution_convert_fusion = bf16[256,3072]{1,0:T(8,128)(2,1)} fusion(bf16[2048,3072]{1,0:T(8,128)(2,1)} %param.13, f32[256,2048]{1,0:T(8,128)} %fusion.13, bf16[256,3072]{1,0:T(8,128)(2,1)S(1)} %bitcast.40, bf16[3072,2048]{1,0:T(8,128)(2,1)} %param.12), kind=kOutput, calls=%fused_computation.1 | convolution fusion | flops 6446383104 | bytes 30408704 | tf_op jit(solution)/shard_map/dot_general | solution.py:13
  72.9 5.9 %all-to-all-start = ((bf16[16,16,3072]{2,1,0:T(8,128)(2,1)}), bf16[16,16,3072]{2,1,0:T(8,128)(2,1)S(1)}, u32[]{:S(2)}, u32[]{:S(2)}) async-start(bf16[16,16,3072]{2,1,0:T(8,128)(2,1)} %bitcast.5), calls=%async_computation | async-start | bytes 3145728 | tf_op jit(solution)/shard_map/all_to_all | solution.py:54
  78.8 0.1 copy.27
  78.9 0.1 reshape.41
  79.0 36.0 %all-to-all-done = bf16[16,16,3072]{2,1,0:T(8,128)(2,1)S(1)} async-done(((bf16[16,16,3072]{2,1,0:T(8,128)(2,1)}), bf16[16,16,3072]{2,1,0:T(8,128)(2,1)S(1)}, u32[]{:S(2)}, u32[]{:S(2)}) %all-to-all-start) | async-done | bytes 1572896 | tf_op jit(solution)/shard_map/all_to_all | solution.py:54
  115.0 0.2 convert_reduce_fusion
  115.3 0.7 gather_fusion
  116.0 0.2 reshape.40
  116.2 0.3 fusion.10
  116.5 0.8 fusion.4
  (30 shorter events, 0.3 us)
Async XLA Ops:
  0.0 3.0 %copy-start = (bf16[16,3072]{1,0:T(8,128)(2,1)S(1)}, bf16[16,3072]{1,0:T(8,128)(2,1)}, u32[]{:S(2)}) copy-start(bf16[16,3072]{1,0:T(8,128)(2,1)} %param.7) | copy-start | bytes 294916
  3.9 4.2 %collective-permute-start = (bf16[1,16,3072]{2,1,0:T(8,128)(2,1)S(1)}, bf16[1,16,3072]{2,1,0:T(8,128)(2,1)S(1)}, u32[]{:S(2)}, u32[]{:S(2)}) collective-permute-start(bf16[1,16,3072]{2,1,0:T(8,128)(2,1)S(1)} %get-tuple-element.21), channel_id=1, source_target_pairs={{0,1},{1,0},{2,3},{3,2},{4,5},{5,4},{6,7},{7,6},{8,9},{9,8},{10,11... | collective-permute-start | bytes 294920 | tf_op jit(solution)/shard_map/ppermute | solution.py:49
  4.7 4.4 %collective-permute-start.1 = (bf16[1,16,3072]{2,1,0:T(8,128)(2,1)S(1)}, bf16[1,16,3072]{2,1,0:T(8,128)(2,1)S(1)}, u32[]{:S(2)}, u32[]{:S(2)}) collective-permute-start(bf16[1,16,3072]{2,1,0:T(8,128)(2,1)S(1)} %get-tuple-element.20), channel_id=1, source_target_pairs={{0,2},{1,3},{2,0},{3,1},{4,6},{5,7},{6,4},{7,5},{8,10},{9,11},{10,... | collective-permute-start | bytes 294920 | tf_op jit(solution)/shard_map/ppermute | solution.py:49
  4.9 6.7 %collective-permute-start.2 = (bf16[1,16,3072]{2,1,0:T(8,128)(2,1)S(1)}, bf16[1,16,3072]{2,1,0:T(8,128)(2,1)S(1)}, u32[]{:S(2)}, u32[]{:S(2)}) collective-permute-start(bf16[1,16,3072]{2,1,0:T(8,128)(2,1)S(1)} %get-tuple-element.19), channel_id=1, source_target_pairs={{0,3},{1,2},{2,1},{3,0},{4,7},{5,6},{6,5},{7,4},{8,11},{9,10},{10,... | collective-permute-start | bytes 294920 | tf_op jit(solution)/shard_map/ppermute | solution.py:49
  6.4 7.6 %collective-permute-start.3 = (bf16[1,16,3072]{2,1,0:T(8,128)(2,1)S(1)}, bf16[1,16,3072]{2,1,0:T(8,128)(2,1)S(1)}, u32[]{:S(2)}, u32[]{:S(2)}) collective-permute-start(bf16[1,16,3072]{2,1,0:T(8,128)(2,1)S(1)} %get-tuple-element.18), channel_id=1, source_target_pairs={{0,4},{1,5},{2,6},{3,7},{4,0},{5,1},{6,2},{7,3},{8,12},{9,13},{10,... | collective-permute-start | bytes 294920 | tf_op jit(solution)/shard_map/ppermute | solution.py:49
  6.5 7.8 %collective-permute-start.4 = (bf16[1,16,3072]{2,1,0:T(8,128)(2,1)S(1)}, bf16[1,16,3072]{2,1,0:T(8,128)(2,1)S(1)}, u32[]{:S(2)}, u32[]{:S(2)}) collective-permute-start(bf16[1,16,3072]{2,1,0:T(8,128)(2,1)S(1)} %get-tuple-element.17), channel_id=1, source_target_pairs={{0,5},{1,4},{2,7},{3,6},{4,1},{5,0},{6,3},{7,2},{8,13},{9,12},{10,... | collective-permute-start | bytes 294920 | tf_op jit(solution)/shard_map/ppermute | solution.py:49
  8.2 8.4 %collective-permute-start.5 = (bf16[1,16,3072]{2,1,0:T(8,128)(2,1)S(1)}, bf16[1,16,3072]{2,1,0:T(8,128)(2,1)S(1)}, u32[]{:S(2)}, u32[]{:S(2)}) collective-permute-start(bf16[1,16,3072]{2,1,0:T(8,128)(2,1)S(1)} %get-tuple-element.16), channel_id=1, source_target_pairs={{0,6},{1,7},{2,4},{3,5},{4,2},{5,3},{6,0},{7,1},{8,14},{9,15},{10,... | collective-permute-start | bytes 294920 | tf_op jit(solution)/shard_map/ppermute | solution.py:49
  9.0 12.6 %collective-permute-start.6 = (bf16[1,16,3072]{2,1,0:T(8,128)(2,1)S(1)}, bf16[1,16,3072]{2,1,0:T(8,128)(2,1)S(1)}, u32[]{:S(2)}, u32[]{:S(2)}) collective-permute-start(bf16[1,16,3072]{2,1,0:T(8,128)(2,1)S(1)} %get-tuple-element.15), channel_id=1, source_target_pairs={{0,7},{1,6},{2,5},{3,4},{4,3},{5,2},{6,1},{7,0},{8,15},{9,14},{10,... | collective-permute-start | bytes 294920 | tf_op jit(solution)/shard_map/ppermute | solution.py:49
  11.6 10.6 %collective-permute-start.7 = (bf16[1,16,3072]{2,1,0:T(8,128)(2,1)S(1)}, bf16[1,16,3072]{2,1,0:T(8,128)(2,1)S(1)}, u32[]{:S(2)}, u32[]{:S(2)}) collective-permute-start(bf16[1,16,3072]{2,1,0:T(8,128)(2,1)S(1)} %get-tuple-element.14), channel_id=1, source_target_pairs={{0,8},{1,9},{2,10},{3,11},{4,12},{5,13},{6,14},{7,15},{8,0},{9,1},... | collective-permute-start | bytes 294920 | tf_op jit(solution)/shard_map/ppermute | solution.py:49
  13.9 16.0 %collective-permute-start.8 = (bf16[1,16,3072]{2,1,0:T(8,128)(2,1)S(1)}, bf16[1,16,3072]{2,1,0:T(8,128)(2,1)S(1)}, u32[]{:S(2)}, u32[]{:S(2)}) collective-permute-start(bf16[1,16,3072]{2,1,0:T(8,128)(2,1)S(1)} %get-tuple-element.13), channel_id=1, source_target_pairs={{0,9},{1,8},{2,11},{3,10},{4,13},{5,12},{6,15},{7,14},{8,1},{9,0},... | collective-permute-start | bytes 294920 | tf_op jit(solution)/shard_map/ppermute | solution.py:49
  14.4 17.7 %collective-permute-start.9 = (bf16[1,16,3072]{2,1,0:T(8,128)(2,1)S(1)}, bf16[1,16,3072]{2,1,0:T(8,128)(2,1)S(1)}, u32[]{:S(2)}, u32[]{:S(2)}) collective-permute-start(bf16[1,16,3072]{2,1,0:T(8,128)(2,1)S(1)} %get-tuple-element.12), channel_id=1, source_target_pairs={{0,10},{1,11},{2,8},{3,9},{4,14},{5,15},{6,12},{7,13},{8,2},{9,3},... | collective-permute-start | bytes 294920 | tf_op jit(solution)/shard_map/ppermute | solution.py:49
  16.5 20.7 %collective-permute-start.10 = (bf16[1,16,3072]{2,1,0:T(8,128)(2,1)S(1)}, bf16[1,16,3072]{2,1,0:T(8,128)(2,1)S(1)}, u32[]{:S(2)}, u32[]{:S(2)}) collective-permute-start(bf16[1,16,3072]{2,1,0:T(8,128)(2,1)S(1)} %get-tuple-element.11), channel_id=1, source_target_pairs={{0,11},{1,10},{2,9},{3,8},{4,15},{5,14},{6,13},{7,12},{8,3},{9,2},... | collective-permute-start | bytes 294920 | tf_op jit(solution)/shard_map/ppermute | solution.py:49
  21.6 20.0 %collective-permute-start.11 = (bf16[1,16,3072]{2,1,0:T(8,128)(2,1)S(1)}, bf16[1,16,3072]{2,1,0:T(8,128)(2,1)S(1)}, u32[]{:S(2)}, u32[]{:S(2)}) collective-permute-start(bf16[1,16,3072]{2,1,0:T(8,128)(2,1)S(1)} %get-tuple-element.10), channel_id=1, source_target_pairs={{0,12},{1,13},{2,14},{3,15},{4,8},{5,9},{6,10},{7,11},{8,4},{9,5},... | collective-permute-start | bytes 294920 | tf_op jit(solution)/shard_map/ppermute | solution.py:49
  22.2 21.9 %collective-permute-start.12 = (bf16[1,16,3072]{2,1,0:T(8,128)(2,1)S(1)}, bf16[1,16,3072]{2,1,0:T(8,128)(2,1)S(1)}, u32[]{:S(2)}, u32[]{:S(2)}) collective-permute-start(bf16[1,16,3072]{2,1,0:T(8,128)(2,1)S(1)} %get-tuple-element.9), channel_id=1, source_target_pairs={{0,13},{1,12},{2,15},{3,14},{4,9},{5,8},{6,11},{7,10},{8,5},{9,4},... | collective-permute-start | bytes 294920 | tf_op jit(solution)/shard_map/ppermute | solution.py:49
  30.0 15.8 %collective-permute-start.13 = (bf16[1,16,3072]{2,1,0:T(8,128)(2,1)S(1)}, bf16[1,16,3072]{2,1,0:T(8,128)(2,1)S(1)}, u32[]{:S(2)}, u32[]{:S(2)}) collective-permute-start(bf16[1,16,3072]{2,1,0:T(8,128)(2,1)S(1)} %get-tuple-element.8), channel_id=1, source_target_pairs={{0,14},{1,15},{2,12},{3,13},{4,10},{5,11},{6,8},{7,9},{8,6},{9,7},... | collective-permute-start | bytes 294920 | tf_op jit(solution)/shard_map/ppermute | solution.py:49
  32.1 16.2 %collective-permute-start.14 = (bf16[1,16,3072]{2,1,0:T(8,128)(2,1)S(1)}, bf16[1,16,3072]{2,1,0:T(8,128)(2,1)S(1)}, u32[]{:S(2)}, u32[]{:S(2)}) collective-permute-start(bf16[1,16,3072]{2,1,0:T(8,128)(2,1)S(1)} %get-tuple-element.7), channel_id=1, source_target_pairs={{0,15},{1,14},{2,13},{3,12},{4,11},{5,10},{6,9},{7,8},{8,7},{9,6},... | collective-permute-start | bytes 294920 | tf_op jit(solution)/shard_map/ppermute | solution.py:49
  72.9 6.1 %copy-start.1 = (f32[16,2]{0,1:T(2,128)S(1)}, f32[16,2]{0,1:T(2,128)}, u32[]{:S(2)}) copy-start(f32[16,2]{0,1:T(2,128)} %param.9) | copy-start | bytes 388
  72.9 42.1 %all-to-all-start = ((bf16[16,16,3072]{2,1,0:T(8,128)(2,1)}), bf16[16,16,3072]{2,1,0:T(8,128)(2,1)S(1)}, u32[]{:S(2)}, u32[]{:S(2)}) async-start(bf16[16,16,3072]{2,1,0:T(8,128)(2,1)} %bitcast.5), calls=%async_computation | async-start | bytes 3145728 | tf_op jit(solution)/shard_map/all_to_all | solution.py:54
